TPU v7x, 32 devices: a whole 2x2x4 slice. The times are simulated.
32 devices in a mesh: ctx: 8 (over y, x, core), tp: 4 (over z).
Axes of the slice: x: 2, y: 2, z: 4, core: 2. Of those that a mesh axis runs over, the one named last changes fastest.
Arguments:
- patches: bfloat16 [4096, 1280], P('ctx'), may hold values from -21 to 21
- window_ids: int32 [4096], P('ctx'), may hold values from -1 to 1023, as said below
- positions: int32 [1024], P('ctx'), may hold values from 0 to 8192, as said below
- text_embed: bfloat16 [8192, 8192], P('ctx', 'tp'), may hold values from -6 to 6
- cotangent: bfloat16 [8192, 8192], P('ctx', 'tp'), may hold values from -0.119628906 to 0.119628906
- qkv_weight: bfloat16 [3, 1280, 1280], P(None, None, 'tp'), may hold values from -0.15625 to 0.15625
- out_weight: bfloat16 [1280, 1280], P('tp'), may hold values from -0.15625 to 0.15625
- merger_weight: bfloat16 [5120, 8192], P('ctx', 'tp'), may hold values from -0.078125 to 0.078125
- norm_gain: bfloat16 [8192], P('tp'), may hold values from 0.099609375 to 1.8984375
Outputs:
- normed: bfloat16 [8192, 8192], P('ctx', 'tp')
- merger_grad: float32 [5120, 8192], P('ctx', 'tp')
Inputs may be any that keep to these rules, and one draw needn't show every extreme that they name: `window_ids`: windows are runs of consecutive patch slots of one index of ctx, each of 4 to 64 slots and a multiple of 4; every window id belongs to one index of ctx; the padding slots of an index of ctx come after its live slots and carry -1. Merged slot j of an index of ctx covers its patch slots 4j to 4j+3 and is live exactly when those are; live slots carry distinct positions, dead ones carry 8192. The live slots of one index of ctx name at most 16 positions among the 1024 positions of any one index of ctx.
All inputs are finite; a program needn't handle non-finite values.
Results may differ from a plain program's by a relative error of at most 0.014.
Values may be sent and summed in bfloat16 or wider, within the bound.
No kernel may reach another device: no remote copies, remote signals or barrier semaphores. Data moves between devices by JAX's collectives and lax.ppermute only.
A program may use at most 128 MiB of HBM per device.

v0:
```python
import jax
import jax.numpy as jnp
from jax import lax
from jax.sharding import PartitionSpec as P

D = 8192
HEAD_DIM = 80


def window_attention(patches, window_ids, qkv_weight):
    slot_rows = patches.shape[0]
    projected = [
        jnp.dot(patches, qkv_weight[i], preferred_element_type=jnp.float32).astype(jnp.bfloat16)
        for i in range(3)
    ]
    local_heads = qkv_weight.shape[2] // HEAD_DIM
    queries = projected[0].reshape(slot_rows, local_heads, HEAD_DIM)
    keys_all = projected[1].reshape(slot_rows, local_heads, HEAD_DIM)
    values = projected[2].reshape(slot_rows, local_heads, HEAD_DIM)
    width = min(512, slot_rows)
    factor = 1.0 / HEAD_DIM**0.5

    def one_block(block_index):
        scores = (
            jnp.einsum("qhd,khd->hqk", queries, keys_all, preferred_element_type=jnp.float32)
            * factor
        )
        allowed = (window_ids[:, None] == window_ids[None, :]) & (window_ids[None, :] >= 0)
        scores = jnp.where(allowed[None], scores, jnp.float32(-1e30))
        highest = jnp.max(scores, axis=2, keepdims=True)
        weights = jnp.exp(scores - highest)
        probs = (weights / jnp.sum(weights, axis=2, keepdims=True)).astype(jnp.bfloat16)
        attended = jnp.einsum("hqk,khd->qhd", probs, values, preferred_element_type=jnp.float32)
        return attended.astype(jnp.bfloat16).reshape(width, local_heads * HEAD_DIM)

    blocks = lax.map(one_block, jnp.arange(slot_rows // width, dtype=jnp.int32))
    return blocks.reshape(slot_rows, local_heads * HEAD_DIM)


def contract_rows(left, right):
    return lax.dot_general(
        left, right, (((0,), (0,)), ((), ())), preferred_element_type=jnp.float32
    )


def shards(
    patches,
    window_ids,
    positions,
    text_embed,
    cotangent,
    qkv_weight,
    out_weight,
    merger_weight,
    norm_gain,
):
    ctx_size = lax.axis_size("ctx")
    slots = positions.shape[0]
    tok_rows = text_embed.shape[0]
    bucket_size = slots // ctx_size
    attended = window_attention(patches, window_ids, qkv_weight)
    partial_out = jnp.dot(attended, out_weight, preferred_element_type=jnp.float32)
    summed = lax.psum(partial_out.astype(jnp.bfloat16), "tp").astype(jnp.float32)
    hidden = (patches.astype(jnp.float32) + summed).astype(jnp.bfloat16)
    merged_in = hidden.reshape(slots, 4 * hidden.shape[1])
    columns = lax.all_to_all(merged_in, "ctx", split_axis=1, concat_axis=0, tiled=True)
    chosen = merged_in
    merged = jnp.dot(
        chosen,
        lax.all_gather(merger_weight, "ctx", axis=0, tiled=True),
        preferred_element_type=jnp.float32,
    ).astype(jnp.bfloat16)
    target = positions // tok_rows
    hits = (target[:, None] == jnp.arange(ctx_size, dtype=jnp.int32)[None, :]).astype(jnp.int32)
    ranks = jnp.sum(jnp.cumsum(hits, axis=0) * hits, axis=1) - 1
    bucket = jnp.where(target < ctx_size, target * bucket_size + ranks, -1)
    select = jnp.arange(slots, dtype=jnp.int32)[:, None] == bucket[None, :]
    select_mat = select.astype(jnp.bfloat16)
    outgoing = jnp.dot(select_mat, merged, preferred_element_type=jnp.float32).astype(jnp.bfloat16)
    local_row = positions % tok_rows
    occupied = jnp.any(select, axis=1)
    out_rows = jnp.where(occupied, jnp.sum(jnp.where(select, local_row[None, :], 0), axis=1), -1)
    incoming, in_rows = (
        lax.all_to_all(outgoing, "ctx", split_axis=0, concat_axis=0, tiled=True),
        lax.all_to_all(out_rows, "ctx", split_axis=0, concat_axis=0, tiled=True),
    )
    placed = jnp.arange(tok_rows, dtype=jnp.int32)[:, None] == in_rows[None, :]
    placed_mat = placed.astype(jnp.bfloat16)
    vision = jnp.dot(placed_mat, incoming, preferred_element_type=jnp.float32)
    is_vision = jnp.any(placed, axis=1)
    embedded = jnp.where(is_vision[:, None], vision, text_embed.astype(jnp.float32))
    gain_vec = norm_gain.astype(jnp.float32)[None, :]
    gained = gain_vec * cotangent.astype(jnp.float32)
    squares, inner = lax.psum(
        (jnp.sum(embedded * embedded, axis=1), jnp.sum(embedded * gained, axis=1)), "tp"
    )
    scale = lax.rsqrt(squares / D + 1e-06)[:, None]
    normed = (embedded * scale * gain_vec).astype(jnp.bfloat16)
    d_embed = (scale * gained - embedded * scale**3 * inner[:, None] / D).astype(jnp.bfloat16)
    back_rows = contract_rows(placed_mat, d_embed).astype(jnp.bfloat16)
    returned = lax.all_to_all(back_rows, "ctx", split_axis=0, concat_axis=0, tiled=True)
    d_merged = contract_rows(select_mat, returned).astype(jnp.bfloat16)
    chosen = columns
    merger_grad = contract_rows(chosen, lax.all_gather(d_merged, "ctx", axis=0, tiled=True))
    return (normed, merger_grad)


def solution(mesh):
    in_specs = (
        P("ctx", None),
        P("ctx"),
        P("ctx"),
        P("ctx", "tp"),
        P("ctx", "tp"),
        P(None, None, "tp"),
        P("tp", None),
        P("ctx", "tp"),
        P("tp"),
    )
    out_specs = (P("ctx", "tp"), P("ctx", "tp"))
    return jax.shard_map(shards, mesh=mesh, in_specs=in_specs, out_specs=out_specs, check_vma=False)
```

profile of v0, /device:TPU:0, one launch (start us, length us, event | category | flops | bytes accessed | tf_op | source)
XLA Modules:
  0.0 256.8 jit_solution(3629582103694238064)
XLA Ops:
  8.1 2.3 convolution_convert_fusion.5
  10.4 2.2 convolution_convert_fusion.4
  12.6 1.8 convolution_convert_fusion.6
  14.4 0.2 compare_and_fusion
  14.6 3.8 %fusion.27 = (f32[4,512]{1,0:T(4,128)S(1)}, f32[4,512,512]{1,2,0:T(8,128)}) fusion(pred[512,512]{0,1:T(8,128)(4,1)S(1)} %compare_and_fusion, bf16[512,4,80]{0,2,1:T(8,128)(2,1)S(1)} %bitcast.45, bf16[512,4,80]{0,2,1:T(8,128)(2,1)S(1)} %bitcast.46), kind=kOutput, calls=%fused_computation.59 | convolution fusion | flops 171966976 | bytes 5120000 | tf_op jit(solution)/shard_map/while/body/eval_jaxpr/sub | solution.py:31
  18.4 2.7 %fusion.8 = bf16[4,80,512]{2,1,0:T(8,128)(2,1)S(1)} fusion(bf16[512,4,80]{0,2,1:T(8,128)(2,1)S(1)} %bitcast.44, f32[4,512,512]{1,2,0:T(8,128)} %get-tuple-element.29, f32[4,512]{1,0:T(4,128)S(1)} %get-tuple-element.28), kind=kOutput, calls=%fused_computation.25 | convolution fusion | flops 170033152 | bytes 4857856 | tf_op jit(solution)/shard_map/while/body/eval_jaxpr/hqk,khd->qhd/dot_general | solution.py:33
  21.1 1.9 convolution_convert_fusion
  23.1 0.5 all-gather.3.cloned.1.call-update
  24.4 0.7 select_n.47
  25.0 5.2 %all-to-all-start = ((s32[8,16,1]{1,2,0:T(1,128)}), s32[8,16,1]{1,2,0:T(1,128)S(1)}, u32[]{:S(2)}, u32[]{:S(2)}) async-start(s32[8,16,1]{1,2,0:T(1,128)} %bitcast), calls=%async_computation | async-start | bytes 8192 | tf_op jit(solution)/shard_map/all_to_all | solution.py:85
  30.2 55.8 %all-reduce.3.cloned.1.call-done = bf16[512,1280]{1,0:T(8,128)(2,1)} async-done(((bf16[512,1280]{1,0:T(8,128)(2,1)}), bf16[512,1280]{1,0:T(8,128)(2,1)}) %all-reduce.3.cloned.1.call-update) | async-done | bytes 1310736 | tf_op jit(solution)/shard_map/psum | solution.py:63
  86.0 1.6 add_convert_fusion
  87.6 0.8 reshape.114
  88.5 47.0 %all-gather.3.cloned.1.call-done = bf16[5120,2048]{1,0:T(8,128)(2,1)} async-done(((bf16[640,2048]{1,0:T(8,128)(2,1)}), bf16[5120,2048]{1,0:T(8,128)(2,1)}) %all-gather.3.cloned.1.call-update) | async-done | bytes 20971536 | tf_op jit(solution)/shard_map/all_gather | solution.py:70
  135.5 10.9 %convolution_convert_fusion.2 = bf16[128,2048]{1,0:T(8,128)(2,1)} fusion(bf16[128,5120]{1,0:T(8,128)(2,1)S(1)} %reshape.114, bf16[5120,2048]{1,0:T(8,128)(2,1)} %all-gather.3.cloned.1.call-done, s32[128]{0:T(128)S(1)} %compare_select_fusion), kind=kOutput, calls=%fused_computation.16 | convolution fusion | flops 2752004096 | bytes 22807040 | tf_op jit(solution)/shard_map/dot_general | solution.py:79
  146.4 3.5 %all-to-all-start.1 = ((bf16[8,16,2048]{2,1,0:T(8,128)(2,1)}), bf16[8,16,2048]{2,1,0:T(8,128)(2,1)S(1)}, u32[]{:S(2)}, u32[]{:S(2)}) async-start(bf16[8,16,2048]{2,1,0:T(8,128)(2,1)} %bitcast.9), calls=%async_computation.1 | async-start | bytes 1048576 | tf_op jit(solution)/shard_map/all_to_all | solution.py:84
  150.0 0.5 broadcast.108
  150.5 0.7 reduce.3
  151.2 0.2 fusion.15
  151.5 8.1 %all-to-all-done.1 = bf16[8,16,2048]{2,1,0:T(8,128)(2,1)S(1)} async-done(((bf16[8,16,2048]{2,1,0:T(8,128)(2,1)}), bf16[8,16,2048]{2,1,0:T(8,128)(2,1)S(1)}, u32[]{:S(2)}, u32[]{:S(2)}) %all-to-all-start.1) | async-done | bytes 524320 | tf_op jit(solution)/shard_map/all_to_all | solution.py:84
  159.5 7.1 %multiply_reduce_fusion = (f32[1024]{0:T(1024)S(1)}, f32[1024]{0:T(1024)S(1)}, f32[1024,2048]{1,0:T(8,128)}) fusion(bf16[1024,2048]{1,0:T(8,128)(2,1)} %param.13, f32[2048]{0:T(1024)S(1)} %convert_element_type.78, bf16[1024,2048]{1,0:T(8,128)(2,1)} %param.12, bf16[128,2048]{1,0:T(8,128)(2,1)S(1)} %bitcast.42, s32[128]{0:T(128)S(1)} %eq.74, ...), kind=kOutput, calls=%fused_computation.2 | convolution fusion | flops 553777152 | bytes 17319424 | tf_op jit(solution)/shard_map/dot_general | solution.py:89
  166.6 12.0 %all-reduce = (f32[1024]{0:T(1024)S(1)}, f32[1024]{0:T(1024)S(1)}) all-reduce(f32[1024]{0:T(1024)S(1)} %get-tuple-element.15, f32[1024]{0:T(1024)S(1)} %get-tuple-element.14), channel_id=1, replica_groups=mesh['ctx'=8,'tp'=4] {'tp'}, use_global_device_ids=true, to_apply=%region_9.10 | all-reduce | flops 2048 | bytes 16384 | tf_op jit(solution)/shard_map/psum | solution.py:94
  178.6 6.2 %fusion.3 = bf16[128,2048]{1,0:T(8,128)(2,1)S(1)} fusion(f32[1024,2048]{1,0:T(8,128)} %get-tuple-element.30, bf16[1024,2048]{1,0:T(8,128)(2,1)} %param.13, f32[1024]{0:T(1024)S(1)} %get-tuple-element.17, f32[1024]{0:T(1024)S(1)} %get-tuple-element.24, f32[2048]{0:T(1024)S(1)} %convert_element_type.78, f32[1024]{0:T(1024)S(1)} %get-tuple-element.25, ...), kind=kOutput, calls=%fused_computation.14 | convolution fusion | flops 554041344 | bytes 13128192 | tf_op jit(solution)/shard_map/dot_general | solution.py:41
  184.8 12.1 %all_to_all.49 = bf16[8,16,2048]{2,1,0:T(8,128)(2,1)S(1)} all-to-all(bf16[8,16,2048]{2,1,0:T(8,128)(2,1)S(1)} %bitcast.43), channel_id=1, replica_groups=mesh['ctx'=8,'tp'=4] {'ctx'}, dimensions={0} | all-to-all | bytes 1048576 | tf_op jit(solution)/shard_map/all_to_all | solution.py:101
  196.9 1.2 convolution_convert_fusion.1
  198.1 0.5 all_to_all.38
  198.6 1.2 copy.19
  199.8 3.6 %all-to-all-start.2 = ((bf16[128,8,640]{2,0,1:T(8,128)(2,1)}), bf16[128,8,640]{2,0,1:T(8,128)(2,1)S(1)}, u32[]{:S(2)}, u32[]{:S(2)}) async-start(bf16[128,8,640]{2,0,1:T(8,128)(2,1)} %copy.19), calls=%async_computation.2 | async-start | bytes 2621440 | tf_op jit(solution)/shard_map/all_to_all | solution.py:66
  203.4 6.2 %multiply_convert_fusion = bf16[1024,2048]{1,0:T(8,128)(2,1)} fusion(f32[1024,2048]{1,0:T(8,128)} %get-tuple-element.30, f32[2048]{0:T(1024)S(1)} %convert_element_type.78, f32[1024]{0:T(1024)S(1)} %get-tuple-element.25), kind=kLoop, calls=%fused_computation.4 | loop fusion | flops 6291456 | bytes 12595200 | tf_op jit(solution)/shard_map/convert_element_type | solution.py:98
  209.6 15.6 %all-to-all-done.2 = bf16[128,8,640]{2,0,1:T(8,128)(2,1)S(1)} async-done(((bf16[128,8,640]{2,0,1:T(8,128)(2,1)}), bf16[128,8,640]{2,0,1:T(8,128)(2,1)S(1)}, u32[]{:S(2)}, u32[]{:S(2)}) %all-to-all-start.2) | async-done | bytes 1310752 | tf_op jit(solution)/shard_map/all_to_all | solution.py:66
  225.2 16.6 %all-gather.5.cloned.1.call-done = bf16[1024,2048]{1,0:T(8,128)(2,1)} async-done(((bf16[128,2048]{1,0:T(8,128)(2,1)}), bf16[1024,2048]{1,0:T(8,128)(2,1)}) %all-gather.5.cloned.1.call-update) | async-done | bytes 4194320 | tf_op jit(solution)/shard_map/all_gather | solution.py:104
  241.8 7.5 %fusion.28 = f32[640,2048]{1,0:T(8,128)} fusion(bf16[1024,640]{1,0:T(8,128)(2,1)S(1)} %bitcast.41, bf16[1024,2048]{1,0:T(8,128)(2,1)} %all-gather.5.cloned.1.call-done), kind=kOutput, calls=%fused_computation.60 | convolution fusion | flops 2684354560 | bytes 10747904 | tf_op jit(solution)/shard_map/dot_general | solution.py:41
  (30 shorter events, 1.0 us)
Async XLA Ops:
  8.0 13.1 %copy-start = (bf16[320,1280]{1,0:T(8,128)(2,1)S(1)}, bf16[320,1280]{1,0:T(8,128)(2,1)}, u32[]{:S(2)}) copy-start(bf16[320,1280]{1,0:T(8,128)(2,1)} %param.15) | copy-start | bytes 2457604
  8.0 4.5 %copy-start.2 = (bf16[512,1280]{1,0:T(8,128)(2,1)S(1)}, bf16[512,1280]{1,0:T(8,128)(2,1)}, u32[]{:S(2)}) copy-start(bf16[512,1280]{1,0:T(8,128)(2,1)} %param.9) | copy-start | bytes 3932164
  8.0 6.3 %copy-start.3 = (s32[512]{0:T(512)S(1)}, s32[512]{0:T(512)}, u32[]{:S(2)}) copy-start(s32[512]{0:T(512)} %param.10) | copy-start | bytes 6148
  8.0 78.0 %all-reduce.3.cloned.1.call-start = ((), (), s32[]{:S(2)}) async-start(), calls=%async_computation.4 | async-start | bytes 2621440 | tf_op jit(solution)/shard_map/psum | solution.py:63
  21.1 2.6 copy-start.5
  23.0 112.5 %all-gather.3.cloned.1.call-start = ((), (), s32[]{:S(2)}) async-start(), calls=%async_computation.5 | async-start | bytes 23592960 | tf_op jit(solution)/shard_map/all_gather | solution.py:70
  25.0 121.4 %all-to-all-start = ((s32[8,16,1]{1,2,0:T(1,128)}), s32[8,16,1]{1,2,0:T(1,128)S(1)}, u32[]{:S(2)}, u32[]{:S(2)}) async-start(s32[8,16,1]{1,2,0:T(1,128)} %bitcast), calls=%async_computation | async-start | bytes 8192 | tf_op jit(solution)/shard_map/all_to_all | solution.py:85
  88.5 61.5 %copy-start.4 = (bf16[2048]{0:T(1024)(128)(2,1)S(1)}, bf16[2048]{0:T(1024)(128)(2,1)}, u32[]{:S(2)}) copy-start(bf16[2048]{0:T(1024)(128)(2,1)} %param.17) | copy-start | bytes 12292
  146.4 13.2 %all-to-all-start.1 = ((bf16[8,16,2048]{2,1,0:T(8,128)(2,1)}), bf16[8,16,2048]{2,1,0:T(8,128)(2,1)S(1)}, u32[]{:S(2)}, u32[]{:S(2)}) async-start(bf16[8,16,2048]{2,1,0:T(8,128)(2,1)} %bitcast.9), calls=%async_computation.1 | async-start | bytes 1048576 | tf_op jit(solution)/shard_map/all_to_all | solution.py:84
  149.9 91.9 %all-gather.5.cloned.1.call-start = ((), (), s32[]{:S(2)}) async-start(), calls=%async_computation.6 | async-start | bytes 4718592 | tf_op jit(solution)/shard_map/all_gather | solution.py:104
  199.8 25.4 %all-to-all-start.2 = ((bf16[128,8,640]{2,0,1:T(8,128)(2,1)}), bf16[128,8,640]{2,0,1:T(8,128)(2,1)S(1)}, u32[]{:S(2)}, u32[]{:S(2)}) async-start(bf16[128,8,640]{2,0,1:T(8,128)(2,1)} %copy.19), calls=%async_computation.2 | async-start | bytes 2621440 | tf_op jit(solution)/shard_map/all_to_all | solution.py:66
  241.8 7.6 %copy-start.1 = (bf16[320,1280]{1,0:T(8,128)(2,1)S(1)}, bf16[320,1280]{1,0:T(8,128)(2,1)}, u32[]{:S(2)}) copy-start(bf16[320,1280]{1,0:T(8,128)(2,1)} %param.15) | copy-start | bytes 2457604
Sparse Core Ops, SparseCore 0:
  23.2 62.7 all-reduce.2
Sparse Core Ops, SparseCore 1:
  25.4 110.0 all-gather.2
  198.2 43.5 all-gather.4
where the time goes:
time: 257 us
  waiting for transfers between devices  144 us (56%)
  matrix products  47.5 us (18%)
  blocking collectives  24.1 us (9%)
  between operations  15.7 us (6%)
  starting transfers between devices  12.4 us (5%)
  other arithmetic  9.6 us (4%)
  local copies, waits for them, and re-layouts  3.84 us (1%)
    psum x1, waiting for transfers between devices, shards(): lax.psum(partial_out.astype(jnp.bfloat16), 'tp').astype(jnp.float32)  55.8 us
    all_gather x1, waiting for transfers between devices, shards(): lax.all_gather(merger_weight, 'ctx', axis=0, tiled=True)  47 us
    all_gather x1, waiting for transfers between devices, shards(): lax.all_gather(d_merged, 'ctx', axis=0, tiled=True)  16.6 us
    all_to_all x1, waiting for transfers between devices, shards(): lax.all_to_all(merged_in, 'ctx', split_axis=1, concat_axis=0, tiled=True)  15.6 us
    dot_general x3, matrix products, contract_rows(): lax.dot_general(left, right, (((0,), (0,)), ((), ())), preferred_element_...  14.9 us
    all_to_all x1, blocking collectives, shards(): lax.all_to_all(back_rows, 'ctx', split_axis=0, concat_axis=0, tiled=True)  12.1 us
    psum x1, blocking collectives, shards(): lax.psum((jnp.sum(embedded * embedded, axis=1), jnp.sum(embedded * gained...  12 us
    dot_general x1, matrix products, shards(): jnp.dot(select_mat, merged, preferred_element_type=jnp.float32)  10.9 us
  transfers between devices with their start and end apart: 6, of which 5 were waited for; matrix products, arithmetic and copies ran while one was open for 9% of the time, Pallas kernels for 0%

commit v1 on v0

--- a/solution.py
+++ b/solution.py
@@ -67,7 +67,9 @@
     chosen = merged_in
     merged = jnp.dot(
         chosen,
-        lax.all_gather(merger_weight, "ctx", axis=0, tiled=True),
+        jnp.concatenate(
+            lax.all_to_all(jnp.stack([merger_weight] * lax.axis_size("ctx")), "ctx", 0, 0), axis=0
+        ),
         preferred_element_type=jnp.float32,
     ).astype(jnp.bfloat16)
     target = positions // tok_rows

time: 257 us -> 378 us (1.47)
  waiting for transfers between devices: 144 us -> 252 us
  local copies, waits for them, and re-layouts: 3.84 us -> 12.3 us
  starting transfers between devices: 12.4 us -> 17.3 us
    all_to_all x0 -> x1, waiting for transfers between devices: none -> 150 us  [shards(): lax.all_to_all(jnp.stack([merger_weight] * lax.axis_size('ctx')), 'ctx',...]
    all_gather x1 -> x0, waiting for transfers between devices: 47 us -> none  [shards(): lax.all_gather(merger_weight, 'ctx', axis=0, tiled=True)]
    another operation x0 -> x1, local copies, waits for them, and re-layouts: none -> 8.45 us  [shards(): jnp.stack([merger_weight] * lax.axis_size('ctx'))]
    all_to_all x0 -> x1, starting transfers between devices: none -> 6.22 us  [shards(): lax.all_to_all(jnp.stack([merger_weight] * lax.axis_size('ctx')), 'ctx',...]
    psum x1, waiting for transfers between devices: 55.8 us -> 61.9 us  [shards(): lax.psum(partial_out.astype(jnp.bfloat16), 'tp').astype(jnp.float32)]
  transfers between devices with their start and end apart: 6 -> 6, of which waited for: 5 -> 5; matrix products, arithmetic and copies ran while one was open for 9% -> 10% of each run, Pallas kernels for 0% -> 0%
where the time goes in v1:
time: 378 us; the launch traced here: 377 us
  waiting for transfers between devices  252 us (67%)
  matrix products  46.4 us (12%)
  blocking collectives  25.2 us (7%)
  starting transfers between devices  17.3 us (5%)
  between operations  14.3 us (4%)
  local copies, waits for them, and re-layouts  12.3 us (3%)
  other arithmetic  9.6 us (3%)
    all_to_all x1, waiting for transfers between devices, shards(): lax.all_to_all(jnp.stack([merger_weight] * lax.axis_size('ctx')), 'ctx',...  150 us
    psum x1, waiting for transfers between devices, shards(): lax.psum(partial_out.astype(jnp.bfloat16), 'tp').astype(jnp.float32)  61.9 us
    all_gather x1, waiting for transfers between devices, shards(): lax.all_gather(d_merged, 'ctx', axis=0, tiled=True)  16.5 us
    all_to_all x1, waiting for transfers between devices, shards(): lax.all_to_all(merged_in, 'ctx', split_axis=1, concat_axis=0, tiled=True)  15.8 us
    dot_general x3, matrix products, contract_rows(): lax.dot_general(left, right, (((0,), (0,)), ((), ())), preferred_element_...  14.9 us
    psum x1, blocking collectives, shards(): lax.psum((jnp.sum(embedded * embedded, axis=1), jnp.sum(embedded * gained...  13.1 us
    all_to_all x1, blocking collectives, shards(): lax.all_to_all(back_rows, 'ctx', split_axis=0, concat_axis=0, tiled=True)  12.1 us
    dot_general x1, matrix products, shards(): jnp.dot(select_mat, merged, preferred_element_type=jnp.float32)  10.8 us
  transfers between devices with their start and end apart: 6, of which 5 were waited for; matrix products, arithmetic and copies ran while one was open for 10% of the time, Pallas kernels for 0%

profile of v1, /device:TPU:0, one launch (start us, length us, event | category | flops | bytes accessed | tf_op | source)
XLA Modules:
  0.0 377.1 jit_solution(14064284301120815800)
XLA Ops:
  7.2 8.5 %stack.2 = bf16[8,640,2048]{2,1,0:T(8,128)(2,1)} broadcast(bf16[640,2048]{1,0:T(8,128)(2,1)} %param.16), dimensions={1,2} | broadcast | bytes 23592960 | tf_op jit(solution)/shard_map/stack | solution.py:71
  15.6 6.2 %all-to-all-start.1 = ((bf16[8,640,2048]{2,1,0:T(8,128)(2,1)}), bf16[8,640,2048]{2,1,0:T(8,128)(2,1)}, u32[]{:S(2)}, u32[]{:S(2)}) async-start(bf16[8,640,2048]{2,1,0:T(8,128)(2,1)} %stack.2), calls=%async_computation.1 | async-start | bytes 41943040 | tf_op jit(solution)/shard_map/all_to_all | solution.py:71
  21.9 0.2 compare_and_fusion
  22.2 1.8 convolution_convert_fusion.5
  24.0 1.8 convolution_convert_fusion.4
  25.7 1.8 convolution_convert_fusion.6
  27.5 3.7 fusion.27
  31.3 2.7 fusion.8
  34.0 1.9 convolution_convert_fusion
  36.6 0.7 select_n.47
  37.3 61.9 %all-reduce.3.cloned.1.call-done = bf16[512,1280]{1,0:T(8,128)(2,1)} async-done(((bf16[512,1280]{1,0:T(8,128)(2,1)}), bf16[512,1280]{1,0:T(8,128)(2,1)}) %all-reduce.3.cloned.1.call-update) | async-done | bytes 1310736 | tf_op jit(solution)/shard_map/psum | solution.py:63
  99.2 1.6 add_convert_fusion
  100.8 0.8 reshape.119
  101.7 149.7 %all-to-all-done.1 = bf16[8,640,2048]{2,1,0:T(8,128)(2,1)} async-done(((bf16[8,640,2048]{2,1,0:T(8,128)(2,1)}), bf16[8,640,2048]{2,1,0:T(8,128)(2,1)}, u32[]{:S(2)}, u32[]{:S(2)}) %all-to-all-start.1) | async-done | bytes 20971552 | tf_op jit(solution)/shard_map/all_to_all | solution.py:71
  251.4 3.3 all-to-all-start
  254.7 10.8 %convolution_convert_fusion.2 = bf16[128,2048]{1,0:T(8,128)(2,1)} fusion(bf16[128,5120]{1,0:T(8,128)(2,1)S(1)} %reshape.119, bf16[5120,2048]{1,0:T(8,128)(2,1)} %bitcast.9, s32[128]{0:T(128)S(1)} %compare_select_fusion), kind=kOutput, calls=%fused_computation.16 | convolution fusion | flops 2752004096 | bytes 22807040 | tf_op jit(solution)/shard_map/dot_general | solution.py:81
  265.5 4.1 %all-to-all-start.2 = ((bf16[8,16,2048]{2,1,0:T(8,128)(2,1)}), bf16[8,16,2048]{2,1,0:T(8,128)(2,1)S(1)}, u32[]{:S(2)}, u32[]{:S(2)}) async-start(bf16[8,16,2048]{2,1,0:T(8,128)(2,1)} %bitcast.10), calls=%async_computation.2 | async-start | bytes 1048576 | tf_op jit(solution)/shard_map/all_to_all | solution.py:86
  269.7 0.5 broadcast.110
  270.2 0.7 reduce.3
  271.2 8.2 %all-to-all-done.2 = bf16[8,16,2048]{2,1,0:T(8,128)(2,1)S(1)} async-done(((bf16[8,16,2048]{2,1,0:T(8,128)(2,1)}), bf16[8,16,2048]{2,1,0:T(8,128)(2,1)S(1)}, u32[]{:S(2)}, u32[]{:S(2)}) %all-to-all-start.2) | async-done | bytes 524320 | tf_op jit(solution)/shard_map/all_to_all | solution.py:86
  279.4 7.0 %multiply_reduce_fusion = (f32[1024]{0:T(1024)S(1)}, f32[1024]{0:T(1024)S(1)}, f32[1024,2048]{1,0:T(8,128)}) fusion(bf16[1024,2048]{1,0:T(8,128)(2,1)} %param.13, f32[2048]{0:T(1024)S(1)} %convert_element_type.78, bf16[1024,2048]{1,0:T(8,128)(2,1)} %param.12, bf16[128,2048]{1,0:T(8,128)(2,1)S(1)} %bitcast.43, s32[128]{0:T(128)S(1)} %eq.74, ...), kind=kOutput, calls=%fused_computation.2 | convolution fusion | flops 553777152 | bytes 17319424 | tf_op jit(solution)/shard_map/dot_general | solution.py:91
  286.4 13.1 %all-reduce = (f32[1024]{0:T(1024)S(1)}, f32[1024]{0:T(1024)S(1)}) all-reduce(f32[1024]{0:T(1024)S(1)} %get-tuple-element.15, f32[1024]{0:T(1024)S(1)} %get-tuple-element.14), channel_id=1, replica_groups=mesh['ctx'=8,'tp'=4] {'tp'}, use_global_device_ids=true, to_apply=%region_9.10 | all-reduce | flops 2048 | bytes 16384 | tf_op jit(solution)/shard_map/psum | solution.py:96
  299.5 6.2 %fusion.3 = bf16[128,2048]{1,0:T(8,128)(2,1)S(1)} fusion(f32[1024,2048]{1,0:T(8,128)} %get-tuple-element.30, bf16[1024,2048]{1,0:T(8,128)(2,1)} %param.13, f32[1024]{0:T(1024)S(1)} %get-tuple-element.17, f32[1024]{0:T(1024)S(1)} %get-tuple-element.24, f32[2048]{0:T(1024)S(1)} %convert_element_type.78, f32[1024]{0:T(1024)S(1)} %get-tuple-element.25, ...), kind=kOutput, calls=%fused_computation.14 | convolution fusion | flops 554041344 | bytes 13128192 | tf_op jit(solution)/shard_map/dot_general | solution.py:41
  305.7 12.1 %all_to_all.54 = bf16[8,16,2048]{2,1,0:T(8,128)(2,1)S(1)} all-to-all(bf16[8,16,2048]{2,1,0:T(8,128)(2,1)S(1)} %bitcast.44), channel_id=1, replica_groups=mesh['ctx'=8,'tp'=4] {'ctx'}, dimensions={0} | all-to-all | bytes 1048576 | tf_op jit(solution)/shard_map/all_to_all | solution.py:103
  317.8 1.2 convolution_convert_fusion.1
  319.0 0.5 all_to_all.42
  319.5 1.2 copy.19
  320.7 3.6 all-to-all-start.3
  324.3 6.2 %multiply_convert_fusion = bf16[1024,2048]{1,0:T(8,128)(2,1)} fusion(f32[1024,2048]{1,0:T(8,128)} %get-tuple-element.30, f32[2048]{0:T(1024)S(1)} %convert_element_type.78, f32[1024]{0:T(1024)S(1)} %get-tuple-element.25), kind=kLoop, calls=%fused_computation.4 | loop fusion | flops 6291456 | bytes 12595200 | tf_op jit(solution)/shard_map/convert_element_type | solution.py:100
  330.5 15.8 %all-to-all-done.3 = bf16[128,8,640]{2,0,1:T(8,128)(2,1)S(1)} async-done(((bf16[128,8,640]{2,0,1:T(8,128)(2,1)}), bf16[128,8,640]{2,0,1:T(8,128)(2,1)S(1)}, u32[]{:S(2)}, u32[]{:S(2)}) %all-to-all-start.3) | async-done | bytes 1310752 | tf_op jit(solution)/shard_map/all_to_all | solution.py:66
  346.3 16.5 %all-gather.2.cloned.1.call-done = bf16[1024,2048]{1,0:T(8,128)(2,1)} async-done(((bf16[128,2048]{1,0:T(8,128)(2,1)}), bf16[1024,2048]{1,0:T(8,128)(2,1)}) %all-gather.2.cloned.1.call-update) | async-done | bytes 4194320 | tf_op jit(solution)/shard_map/all_gather | solution.py:106
  362.7 7.5 %fusion.28 = f32[640,2048]{1,0:T(8,128)} fusion(bf16[1024,640]{1,0:T(8,128)(2,1)S(1)} %bitcast.42, bf16[1024,2048]{1,0:T(8,128)(2,1)} %all-gather.2.cloned.1.call-done), kind=kOutput, calls=%fused_computation.60 | convolution fusion | flops 2684354560 | bytes 10747904 | tf_op jit(solution)/shard_map/dot_general | solution.py:41
  (30 shorter events, 1.1 us)
Async XLA Ops:
  7.2 26.8 %copy-start = (bf16[320,1280]{1,0:T(8,128)(2,1)S(1)}, bf16[320,1280]{1,0:T(8,128)(2,1)}, u32[]{:S(2)}) copy-start(bf16[320,1280]{1,0:T(8,128)(2,1)} %param.15) | copy-start | bytes 2457604
  15.6 6.3 %copy-start.3 = (s32[512]{0:T(512)S(1)}, s32[512]{0:T(512)}, u32[]{:S(2)}) copy-start(s32[512]{0:T(512)} %param.10) | copy-start | bytes 6148
  15.6 6.6 %copy-start.2 = (bf16[512,1280]{1,0:T(8,128)(2,1)S(1)}, bf16[512,1280]{1,0:T(8,128)(2,1)}, u32[]{:S(2)}) copy-start(bf16[512,1280]{1,0:T(8,128)(2,1)} %param.9) | copy-start | bytes 3932164
  15.6 235.7 %all-to-all-start.1 = ((bf16[8,640,2048]{2,1,0:T(8,128)(2,1)}), bf16[8,640,2048]{2,1,0:T(8,128)(2,1)}, u32[]{:S(2)}, u32[]{:S(2)}) async-start(bf16[8,640,2048]{2,1,0:T(8,128)(2,1)} %stack.2), calls=%async_computation.1 | async-start | bytes 41943040 | tf_op jit(solution)/shard_map/all_to_all | solution.py:71
  21.9 77.3 %all-reduce.3.cloned.1.call-start = ((), (), s32[]{:S(2)}) async-start(), calls=%async_computation.5 | async-start | bytes 2621440 | tf_op jit(solution)/shard_map/psum | solution.py:63
  31.3 4.7 %copy-start.5 = (s32[128]{0:T(128)S(1)}, s32[128]{0:T(128)}, u32[]{:S(2)}) copy-start(s32[128]{0:T(128)} %param.11) | copy-start | bytes 1540
  251.4 14.1 %all-to-all-start = ((s32[8,16,1]{1,2,0:T(1,128)}), s32[8,16,1]{1,2,0:T(1,128)S(1)}, u32[]{:S(2)}, u32[]{:S(2)}) async-start(s32[8,16,1]{1,2,0:T(1,128)} %bitcast), calls=%async_computation | async-start | bytes 8192 | tf_op jit(solution)/shard_map/all_to_all | solution.py:87
  254.7 15.0 %copy-start.4 = (bf16[2048]{0:T(1024)(128)(2,1)S(1)}, bf16[2048]{0:T(1024)(128)(2,1)}, u32[]{:S(2)}) copy-start(bf16[2048]{0:T(1024)(128)(2,1)} %param.17) | copy-start | bytes 12292
  265.5 13.8 %all-to-all-start.2 = ((bf16[8,16,2048]{2,1,0:T(8,128)(2,1)}), bf16[8,16,2048]{2,1,0:T(8,128)(2,1)S(1)}, u32[]{:S(2)}, u32[]{:S(2)}) async-start(bf16[8,16,2048]{2,1,0:T(8,128)(2,1)} %bitcast.10), calls=%async_computation.2 | async-start | bytes 1048576 | tf_op jit(solution)/shard_map/all_to_all | solution.py:86
  269.6 93.1 %all-gather.2.cloned.1.call-start = ((), (), s32[]{:S(2)}) async-start(), calls=%async_computation.6 | async-start | bytes 4718592 | tf_op jit(solution)/shard_map/all_gather | solution.py:106
  320.7 25.5 %all-to-all-start.3 = ((bf16[128,8,640]{2,0,1:T(8,128)(2,1)}), bf16[128,8,640]{2,0,1:T(8,128)(2,1)S(1)}, u32[]{:S(2)}, u32[]{:S(2)}) async-start(bf16[128,8,640]{2,0,1:T(8,128)(2,1)} %copy.19), calls=%async_computation.3 | async-start | bytes 2621440 | tf_op jit(solution)/shard_map/all_to_all | solution.py:66
  362.7 7.5 %copy-start.1 = (bf16[320,1280]{1,0:T(8,128)(2,1)S(1)}, bf16[320,1280]{1,0:T(8,128)(2,1)}, u32[]{:S(2)}) copy-start(bf16[320,1280]{1,0:T(8,128)(2,1)} %param.15) | copy-start | bytes 2457604
Sparse Core Ops, SparseCore 0:
  36.0 63.1 all-reduce.2
  319.2 43.5 all-gather.1
